TPU v7x, 32 devices: a whole 2x2x4 slice. The times are simulated.
32 devices in a mesh: orb: 8 (over y, x, core), pan: 4 (over z).
Axes of the slice: x: 2, y: 2, z: 4, core: 2. Of those that a mesh axis runs over, the one named last changes fastest.
Arguments:
- orbitals: float32 [128, 110592], P(('orb', 'pan')), may hold values from -6 to 6
- potential: float32 [110592], replicated, may hold values from -1 to 2
- magic_taps: float32 [16], replicated, may hold values from -4 to 4
- kinetic_taps: float32 [29], replicated, may hold values from -3 to 3
Outputs:
- gradient: float32 [128, 110592], P(('orb', 'pan'))
All inputs are finite; a program needn't handle non-finite values.
Results may differ from a plain program's by a relative error of at most 0.00013.
Values sent between devices are 32-bit elements; how exact they have to be, the bound alone decides.
A program may use at most 128 MiB of HBM per device.

v0:
```python
import functools

import jax
import jax.numpy as jnp
import numpy as np
from jax import lax
from jax.experimental import pallas as pl
from jax.experimental.pallas import tpu as pltpu
from jax.sharding import PartitionSpec as P

G = 48
NC = 110592


def filter_matrix(tap_values, extent):
    tap_count = tap_values.shape[0]
    centre = (tap_count - 1) // 2
    tap_ids = lax.broadcasted_iota(jnp.int32, (tap_count, extent, extent), 0)
    row_ids = lax.broadcasted_iota(jnp.int32, (tap_count, extent, extent), 1)
    col_ids = lax.broadcasted_iota(jnp.int32, (tap_count, extent, extent), 2)
    offset = (col_ids - row_ids - (tap_ids - centre)) % extent
    return jnp.sum(jnp.where(offset == 0, tap_values[:, None, None], jnp.float32(0.0)), axis=0)


def along(matrix, volume, which_axis):
    patterns = {1: "ab,nbcd->nacd", 2: "ab,ncbd->ncad", 3: "ab,ncdb->ncda"}
    return jnp.einsum(patterns[which_axis], matrix, volume, precision=lax.Precision.HIGHEST)


def hamiltonian(block, potential, magic_matrix, kinetic_matrix):
    count_here = block.shape[0]
    volume = block.reshape(count_here, G, G, G)
    smooth = volume
    for which_axis in (1, 2, 3):
        smooth = along(magic_matrix, smooth, which_axis)
    smooth = smooth * potential.reshape(1, G, G, G)
    for which_axis in (1, 2, 3):
        smooth = along(magic_matrix.T, smooth, which_axis)
    kinetic_part = (
        along(kinetic_matrix, volume, 1)
        + along(kinetic_matrix, volume, 2)
        + along(kinetic_matrix, volume, 3)
    )
    return (smooth + kinetic_part).reshape(count_here, G * G * G)


def margin_terms(left, right):
    return jnp.einsum("jc,ic->ji", left, right, precision=lax.Precision.HIGHEST) * (1.0 / NC)


def rotate(margin, panel):
    return jnp.einsum("ji,jc->ic", margin, panel, precision=lax.Precision.HIGHEST)


def plain_shards(orbitals, potential, magic_taps, kinetic_taps):
    magic_matrix = filter_matrix(magic_taps, G)
    kinetic_matrix = filter_matrix(kinetic_taps, G)
    hpsi = hamiltonian(orbitals, potential, magic_matrix, kinetic_matrix)
    psi_cols, hpsi_cols = (
        lax.all_to_all(orbitals, "orb", split_axis=1, concat_axis=0, tiled=True),
        lax.all_to_all(hpsi, "orb", split_axis=1, concat_axis=0, tiled=True),
    )
    psi_every = lax.all_gather(psi_cols, "pan", axis=0, tiled=True)
    margin = lax.psum(margin_terms(psi_every, hpsi_cols), "orb")
    grad_cols = hpsi_cols - rotate(margin, psi_every)
    gradient = lax.all_to_all(grad_cols, "orb", split_axis=0, concat_axis=1, tiled=True)
    return gradient


BF = jnp.bfloat16
F32 = jnp.float32
UNIT = 8
CHUNK = UNIT * G
PARTS = G // UNIT
PER = 2


def split(value):
    high = value.astype(BF)
    return high, (value - high.astype(F32)).astype(BF)


def mul(left, right):
    return jnp.dot(left, right, preferred_element_type=F32)


def pick(rows3, matrix, cols):
    first = matrix.astype(BF)
    rest = matrix - first.astype(F32)
    second = rest.astype(BF)
    third = (rest - second.astype(F32)).astype(BF)
    stack = jnp.concatenate([mul(piece, cols).astype(BF) for piece in (first, second, third)], axis=0)
    return mul(rows3, stack)


def one_hot(values, repeat=1):
    hot = (np.asarray(values)[:, None] % G == np.arange(G)[None, :]).astype(np.float32)
    return jnp.asarray(np.concatenate([hot] * repeat, axis=1), dtype=BF)


def block_range(tap_count):
    centre = (tap_count - 1) // 2
    reach = max(centre, tap_count - 1 - centre)
    return -(-reach // UNIT)


def kernel(n, n_pan, own, cols, n_mag, n_kin,
           psi_ref, v_ref, mats_ref, ez3_ref, ezt_ref, ey3_ref, eyt_ref, ex3_ref, ext_ref, same_ref,
           out_ref,
           wfh, wfl, wbh, wbl, wkh, wkl, xl1, xl2, xb1, sh, sl, xs, kx, kyz, tt, vs,
           hbuf, pc, hc, pm_h, pm_l, hm, gbuf, mp, red, mrow, mall,
           psend, precv, hsend, hrecv, rsend, rrecv, bsend, brecv, gsend, grecv, lsem):
    me = lax.axis_index("orb") * n_pan + lax.axis_index("pan")
    total = n * own
    rows = G * own

    def coords(index):
        return {"orb": lax.div(index, n_pan), "pan": lax.rem(index, n_pan)}

    def each(action):
        def step(k, carry):
            action(lax.rem(me + k, n))
            return carry
        lax.fori_loop(1, n, step, 0)

    def sender(src, dst, send, recv):
        def copy(t):
            return pltpu.make_async_remote_copy(
                src_ref=src(t), dst_ref=dst(me), send_sem=send.at[t], recv_sem=recv.at[me],
                device_id=coords(t), device_id_type=pl.DeviceIdType.MESH)

        def arrival(t):
            return pltpu.make_async_remote_copy(
                src_ref=src(t), dst_ref=dst(t), send_sem=send.at[t], recv_sem=recv.at[t],
                device_id=coords(t), device_id_type=pl.DeviceIdType.MESH)
        return (lambda: each(lambda t: copy(t).start()),
                lambda: each(lambda t: arrival(t).wait_recv()),
                lambda: each(lambda t: copy(t).wait_send()))

    def col_slice(ref, t):
        return ref.at[:, pl.ds(pl.multiple_of(t * cols, 128), cols)]

    barrier = pltpu.get_barrier_semaphore()
    each(lambda t: pl.semaphore_signal(barrier, inc=1, device_id=coords(t), device_id_type=pl.DeviceIdType.MESH))
    pl.semaphore_wait(barrier, n - 1)

    p_start, p_arrive, p_sent = sender(lambda t: col_slice(psi_ref, t), lambda t: pc.at[t], psend, precv)
    h_start, h_arrive, h_sent = sender(lambda t: hbuf.at[t], lambda t: hc.at[t], hsend, hrecv)
    r_start, r_arrive, r_sent = sender(lambda t: mp.at[t], lambda t: red.at[t], rsend, rrecv)
    b_start, b_arrive, b_sent = sender(lambda t: mrow, lambda t: mall.at[t], bsend, brecv)
    g_start, g_arrive, g_sent = sender(lambda t: gbuf.at[t], lambda t: col_slice(out_ref, t), gsend, grecv)

    p_start()
    own_psi = pltpu.make_async_copy(col_slice(psi_ref, me), pc.at[me], lsem.at[0])
    own_psi.start()

    fm, fmt, fk, fkt = (mats_ref[i] for i in range(4))
    ez3, ezt = ez3_ref[...], ezt_ref[...]
    eyt = eyt_ref[...]
    halo = max(n_mag, n_kin)
    z_fwd, z_bwd, z_kin = (pick(ez3, m, ezt) for m in (fmt, fm, fkt))
    same_z = mul(ez3[:, :G], ezt)
    same_y = mul(ey3_ref[halo, :, :G], eyt)
    for reach, matrix, z_part, high, low in (
        (n_mag, fmt, z_fwd, wfh, wfl), (n_mag, fm, z_bwd, wbh, wbl), (n_kin, fkt, None, wkh, wkl)):
        for d in range(-reach, reach + 1):
            y_part = pick(ey3_ref[d + halo], matrix, eyt)
            if z_part is not None:
                block = y_part * z_part
            else:
                block = y_part * same_z
                if d == 0:
                    block = block + same_y * z_kin
            at = pl.ds((d + reach) * CHUNK, CHUNK)
            high[at, :], low[at, :] = split(block)
    ex3, ext = ex3_ref[...], ext_ref[...]
    same = same_ref[...]
    mh, ml = split(pick(ex3, fm, ext) * same)
    kh, kl = split(pick(ex3, fk, ext) * same)
    nh, nl = split(pick(ex3, fmt, ext) * same)
    for i, piece in enumerate((mh, ml, kh, kl)):
        xl1[i * rows:(i + 1) * rows, :] = piece
    for i, piece in enumerate((mh, kh)):
        xl2[i * rows:(i + 1) * rows, :] = piece
    for i, piece in enumerate((nh, nl)):
        xb1[i * rows:(i + 1) * rows, :] = piece

    plane = G * G
    for x in range(G):
        xs[x * own:(x + 1) * own, :] = psi_ref[:, x * plane:(x + 1) * plane]

    def fill(c, value):
        high, low = split(value)
        for e in range(PARTS + 2 * halo):
            if (e - halo) % PARTS == c:
                sh[e * rows:(e + 1) * rows, :] = high
                sl[e * rows:(e + 1) * rows, :] = low
        return high, low

    def planes(reach, high, low, finish):
        def step(i, carry):
            def left(ref):
                return jnp.concatenate(
                    [ref[pl.ds(pl.multiple_of((i * PER + d + halo) * rows, 16), PER * rows), :]
                     for d in range(-reach, reach + 1)], axis=1)
            left_h, left_l = left(sh), left(sl)
            value = mul(left_h, high[...]) + mul(left_h, low[...]) + mul(left_l, high[...])
            finish(pl.ds(pl.multiple_of(i * PER * rows, 8), PER * rows), value)
            return carry
        lax.fori_loop(0, PARTS // PER, step, 0)

    def put(ref):
        def finish(at, value):
            ref[at, :] = value
        return finish

    v_first = v_ref[...].astype(BF)
    v_rest = v_ref[...] - v_first.astype(F32)
    v_second = v_rest.astype(BF)
    v_third = (v_rest - v_second.astype(F32)).astype(BF)
    v_stack = jnp.concatenate([v_first, v_second, v_third], axis=0)
    for c in range(PARTS):
        lanes = slice(c * CHUNK, (c + 1) * CHUNK)
        vs[c * rows:(c + 1) * rows, :] = mul(ex3, v_stack[:, lanes])
        fill(c, xs[:, lanes])
    planes(n_kin, wkh, wkl, put(kyz))
    for c in range(PARTS):
        high, low = split(xs[:, c * CHUNK:(c + 1) * CHUNK])
        one = mul(xl1[...], high)
        two = mul(xl2[...], low)
        fill(c, one[:rows] + one[rows:2 * rows] + two[:rows])
        kx[c * rows:(c + 1) * rows, :] = one[2 * rows:3 * rows] + one[3 * rows:] + two[rows:]

    def with_potential(at, value):
        tt[at, :] = value * vs[at, :]
    planes(n_mag, wfh, wfl, with_potential)
    for c in range(PARTS):
        fill(c, tt[c * rows:(c + 1) * rows, :])
    planes(n_mag, wbh, wbl, put(tt))
    for c in range(PARTS):
        at = slice(c * rows, (c + 1) * rows)
        high, low = split(tt[at, :])
        one = mul(xb1[...], high)
        xs[:, c * CHUNK:(c + 1) * CHUNK] = (
            one[:rows] + one[rows:] + mul(xb1[:rows, :], low) + kx[at, :] + kyz[at, :])
    for x in range(G):
        at, stop = x * plane, (x + 1) * plane
        while at < stop:
            d = at // cols
            until = min(stop, (d + 1) * cols)
            hbuf[d, :, at - d * cols:until - d * cols] = xs[
                x * own:(x + 1) * own, at - x * plane:until - x * plane]
            at = until

    h_start()
    own_h = pltpu.make_async_copy(hbuf.at[me], hc.at[me], lsem.at[1])
    own_h.start()

    own_psi.wait()
    p_arrive()
    for t in range(n):
        hm[t * own:(t + 1) * own, :] = pc[t]
    pm_h[...], pm_l[...] = split(hm[...])

    own_h.wait()
    h_arrive()
    for t in range(n):
        hm[t * own:(t + 1) * own, :] = hc[t]
    h_high, h_low = split(hm[...])
    nt = (((1,), (1,)), ((), ()))

    def mul_t(left, right):
        return lax.dot_general(left, right, nt, preferred_element_type=F32)
    part = (mul_t(h_high, pm_h[...]) + mul_t(h_high, pm_l[...]) + mul_t(h_low, pm_h[...])) * (1.0 / NC)
    for t in range(n):
        mp[t] = part[t * own:(t + 1) * own, :]

    r_start()
    own_m = pltpu.make_async_copy(mp.at[me], red.at[me], lsem.at[2])
    own_m.start()
    own_m.wait()
    r_arrive()
    mrow[...] = jnp.sum(red[...], axis=0)
    b_start()
    own_r = pltpu.make_async_copy(mrow, mall.at[me], lsem.at[3])
    own_r.start()
    own_r.wait()
    b_arrive()
    margin_t = jnp.concatenate([mall[t] for t in range(n)], axis=0)
    m_high, m_low = split(margin_t)
    hm[...] = hm[...] - (mul(m_high, pm_h[...]) + mul(m_high, pm_l[...]) + mul(m_low, pm_h[...]))
    for t in range(n):
        gbuf[t] = hm[t * own:(t + 1) * own, :]
    g_start()
    own_g = pltpu.make_async_copy(gbuf.at[me], col_slice(out_ref, me), lsem.at[4])
    own_g.start()
    own_g.wait()
    p_sent()
    h_sent()
    r_sent()
    b_sent()
    g_arrive()
    g_sent()


def shards(n, n_pan, orbitals, potential, magic_taps, kinetic_taps):
    own, width = orbitals.shape
    cols = width // n
    rows, total = G * own, n * own
    magic_matrix = filter_matrix(magic_taps, G)
    kinetic_matrix = filter_matrix(kinetic_taps, G)
    mats = jnp.stack([magic_matrix, magic_matrix.T, kinetic_matrix, kinetic_matrix.T])
    n_mag, n_kin = block_range(magic_taps.shape[0]), block_range(kinetic_taps.shape[0])
    halo = max(n_mag, n_kin)
    lane = np.arange(CHUNK)
    ez3, ezt = one_hot(lane, 3), one_hot(lane).T
    ey3 = jnp.stack([one_hot(lane // G + UNIT * d, 3) for d in range(-halo, halo + 1)])
    eyt = one_hot(lane // G).T
    row = np.arange(rows)
    ex3, ext = one_hot(row // own, 3), one_hot(row // own).T
    same = jnp.asarray((row[:, None] % own == row[None, :] % own).astype(np.float32))
    vmem = pl.BlockSpec(memory_space=pltpu.VMEM)
    span_m, span_k = (2 * n_mag + 1) * CHUNK, (2 * n_kin + 1) * CHUNK
    chunked = pltpu.VMEM((PARTS * rows, CHUNK), F32)
    halved = pltpu.VMEM(((PARTS + 2 * halo) * rows, CHUNK), BF)
    blocks = pltpu.VMEM((n, own, cols), F32)
    dma = pltpu.SemaphoreType.DMA
    return pl.pallas_call(
        functools.partial(kernel, n, n_pan, own, cols, n_mag, n_kin),
        out_shape=jax.ShapeDtypeStruct((own, width), F32),
        in_specs=[vmem] * 10,
        out_specs=pl.BlockSpec(memory_space=OUT_SPACE),
        scratch_shapes=[
            pltpu.VMEM((span_m, CHUNK), BF), pltpu.VMEM((span_m, CHUNK), BF),
            pltpu.VMEM((span_m, CHUNK), BF), pltpu.VMEM((span_m, CHUNK), BF),
            pltpu.VMEM((span_k, CHUNK), BF), pltpu.VMEM((span_k, CHUNK), BF),
            pltpu.VMEM((4 * rows, rows), BF), pltpu.VMEM((2 * rows, rows), BF), pltpu.VMEM((2 * rows, rows), BF),
            halved, halved,
            pltpu.VMEM((rows, G * G), F32), chunked, chunked, chunked, chunked,
            blocks, blocks, blocks,
            pltpu.VMEM((total, cols), BF), pltpu.VMEM((total, cols), BF), pltpu.VMEM((total, cols), F32),
            blocks,
            pltpu.VMEM((n, own, total), F32), pltpu.VMEM((n, own, total), F32),
            pltpu.VMEM((own, total), F32), pltpu.VMEM((n, own, total), F32),
            dma((n,)), dma((n,)), dma((n,)), dma((n,)), dma((n,)), dma((n,)), dma((n,)), dma((n,)),
            dma((n,)), dma((n,)), dma((5,)),
        ],
        compiler_params=pltpu.CompilerParams(
            collective_id=0, has_side_effects=True, vmem_limit_bytes=60 * 1024 * 1024),
    )(orbitals, potential.reshape(G, G * G), mats, ez3, ezt, ey3, eyt, ex3, ext, same)


OUT_SPACE = pl.ANY


def solution(mesh):
    placed = (P(("orb", "pan"), None), P(), P(), P())
    n_pan = mesh.shape["pan"]
    n = mesh.shape["orb"] * n_pan
    aligned = NC % (n * 128) == 0
    body = functools.partial(shards, n, n_pan) if aligned else plain_shards
    return jax.shard_map(
        body, mesh=mesh, in_specs=placed, out_specs=P(("orb", "pan"), None), check_vma=False
    )
```

profile of v0, /device:TPU:0, one launch (start us, length us, event | category | flops | bytes accessed | tf_op | source)
XLA Modules:
  0.0 149.6 jit_solution(14139496612251733966)
XLA Ops:
  0.0 1.2 select_reduce_fusion
  1.2 1.0 select_reduce_fusion.1
  2.2 0.1 copy.18
  2.3 0.1 copy.19
  2.3 0.7 pad_maximum_fusion.mats_ref
  3.0 1.8 %reshape.5.v_ref = f32[48,2304]{1,0:T(8,128)} reshape(f32[110592]{0:T(1024)} %param.16) | data formatting | bytes 884736 | tf_op jit(solution)/shard_map/reshape | solution.py:350
  4.8 141.9 %shard_map.145 = f32[4,110592]{1,0:T(4,128)} custom-call(f32[4,110592]{1,0:T(4,128)} %psi_ref.1, f32[48,2304]{1,0:T(8,128)} %reshape.5.v_ref, f32[4,48,48]{2,1,0:T(8,128)} %pad_maximum_fusion.mats_ref, bf16[384,144]{1,0:T(8,128)(2,1)} %constant.50.clone.ez3_ref, bf16[48,384]{1,0:T(8,128)(2,1)} %constant.62.ezt_ref, bf16[5,384,144]{2,1,0:T(8,128)(2,1)} %constant.68.ey3_ref, ...), custom_call_target="tpu_custom_call" | custom-call | tf_op jit(solution)/shard_map/pallas_call | solution.py:328
  146.8 2.8 %copy.21 = f32[4,110592]{1,0:T(4,128)} copy(f32[4,110592]{1,0:T(4,128)} %shard_map.145) | data formatting | bytes 3538944
  (2 shorter events, 0.0 us)
where the time goes:
time: 150 us
  Pallas kernels  142 us (95%)
  local copies, waits for them, and re-layouts  4.79 us (3%)
  other arithmetic  2.83 us (2%)
    pallas_call x1, Pallas kernels, shards(): pl.pallas_call(functools.partial(kernel, n, n_pan, own, cols, n_mag, n_ki...  142 us

commit v1 on v0

--- a/solution.py
+++ b/solution.py
@@ -104,57 +104,83 @@
     return -(-reach // UNIT)
 
 
-def kernel(n, n_pan, own, cols, n_mag, n_kin,
-           psi_ref, v_ref, mats_ref, ez3_ref, ezt_ref, ey3_ref, eyt_ref, ex3_ref, ext_ref, same_ref,
+def filter_of(tap_ref, tap_count, flip):
+    centre = (tap_count - 1) // 2
+    row_ids = lax.broadcasted_iota(jnp.int32, (G, G), 0)
+    col_ids = lax.broadcasted_iota(jnp.int32, (G, G), 1)
+    offset = row_ids - col_ids if flip else col_ids - row_ids
+    total = jnp.zeros((G, G), F32)
+    for k in range(tap_count):
+        shift = (k - centre) % G
+        hit = (offset == shift) | (offset == shift - G)
+        total = total + jnp.where(hit, tap_ref[k], 0.0)
+    return total
+
+
+def kernel(n_orb, n_pan, own, cols, n_mag, n_kin,
+           psi_ref, v_ref, mag_ref, kin_ref, ez3_ref, ezt_ref, ey3_ref, eyt_ref, ex3_ref, ext_ref, same_ref,
            out_ref,
-           wfh, wfl, wbh, wbl, wkh, wkl, xl1, xl2, xb1, sh, sl, xs, kx, kyz, tt, vs,
-           hbuf, pc, hc, pm_h, pm_l, hm, gbuf, mp, red, mrow, mall,
+           wfh, wfl, wbh, wbl, wkh, wkl, xl1, xl2, xb1, sh, sl, xs, kx, kyz, tt, vs, vrows,
+           hbuf, pc, hc, pm_h, pm_l, pf, hm, gbuf, mp, red, mrow, mall,
            psend, precv, hsend, hrecv, rsend, rrecv, bsend, brecv, gsend, grecv, lsem):
-    me = lax.axis_index("orb") * n_pan + lax.axis_index("pan")
+    half = n_pan // 2
+    n, n_half = n_orb * n_pan, n_orb * half
+    orb, pan = lax.axis_index("orb"), lax.axis_index("pan")
+    side = lax.div(pan, half)
+    me = orb * n_pan + pan
+    member = orb * half + lax.rem(pan, half)
     total = n * own
     rows = G * own
 
-    def coords(index):
-        return {"orb": lax.div(index, n_pan), "pan": lax.rem(index, n_pan)}
-
-    def each(action):
+    def at_all(t):
+        return {"orb": lax.div(t, n_pan), "pan": lax.rem(t, n_pan)}
+
+    def at_half(t):
+        return {"orb": lax.div(t, half), "pan": side * half + lax.rem(t, half)}
+
+    def block_of(t):
+        return lax.div(t, n_pan) * half + lax.rem(lax.rem(t, n_pan), half)
+
+    def each(action, count=n, first=me):
         def step(k, carry):
-            action(lax.rem(me + k, n))
+            action(lax.rem(first + k, count))
             return carry
-        lax.fori_loop(1, n, step, 0)
-
-    def sender(src, dst, send, recv):
+        lax.fori_loop(1, count, step, 0)
+
+    def sender(src, dst, send, recv, count=n_half, mine=member, coords=at_half):
         def copy(t):
             return pltpu.make_async_remote_copy(
-                src_ref=src(t), dst_ref=dst(me), send_sem=send.at[t], recv_sem=recv.at[me],
+                src_ref=src(t), dst_ref=dst(mine), send_sem=send.at[t], recv_sem=recv.at[mine],
                 device_id=coords(t), device_id_type=pl.DeviceIdType.MESH)
 
         def arrival(t):
             return pltpu.make_async_remote_copy(
                 src_ref=src(t), dst_ref=dst(t), send_sem=send.at[t], recv_sem=recv.at[t],
                 device_id=coords(t), device_id_type=pl.DeviceIdType.MESH)
-        return (lambda: each(lambda t: copy(t).start()),
-                lambda: each(lambda t: arrival(t).wait_recv()),
-                lambda: each(lambda t: copy(t).wait_send()))
-
-    def col_slice(ref, t):
-        return ref.at[:, pl.ds(pl.multiple_of(t * cols, 128), cols)]
+        return (lambda: each(lambda t: copy(t).start(), count, mine),
+                lambda: each(lambda t: arrival(t).wait_recv(), count, mine),
+                lambda: each(lambda t: copy(t).wait_send(), count, mine))
+
+    def col_slice(ref, block):
+        return ref.at[:, pl.ds(pl.multiple_of(block * cols, 128), cols)]
 
     barrier = pltpu.get_barrier_semaphore()
-    each(lambda t: pl.semaphore_signal(barrier, inc=1, device_id=coords(t), device_id_type=pl.DeviceIdType.MESH))
+    each(lambda t: pl.semaphore_signal(barrier, inc=1, device_id=at_all(t), device_id_type=pl.DeviceIdType.MESH))
     pl.semaphore_wait(barrier, n - 1)
 
-    p_start, p_arrive, p_sent = sender(lambda t: col_slice(psi_ref, t), lambda t: pc.at[t], psend, precv)
+    p_start, p_arrive, p_sent = sender(
+        lambda t: col_slice(psi_ref, block_of(t)), lambda t: pc.at[t], psend, precv, n, me, at_all)
     h_start, h_arrive, h_sent = sender(lambda t: hbuf.at[t], lambda t: hc.at[t], hsend, hrecv)
     r_start, r_arrive, r_sent = sender(lambda t: mp.at[t], lambda t: red.at[t], rsend, rrecv)
     b_start, b_arrive, b_sent = sender(lambda t: mrow, lambda t: mall.at[t], bsend, brecv)
     g_start, g_arrive, g_sent = sender(lambda t: gbuf.at[t], lambda t: col_slice(out_ref, t), gsend, grecv)
 
     p_start()
-    own_psi = pltpu.make_async_copy(col_slice(psi_ref, me), pc.at[me], lsem.at[0])
+    own_psi = pltpu.make_async_copy(col_slice(psi_ref, member), pc.at[me], lsem.at[0])
     own_psi.start()
 
-    fm, fmt, fk, fkt = (mats_ref[i] for i in range(4))
+    fm, fmt = (filter_of(mag_ref, mag_ref.shape[0], flip) for flip in (False, True))
+    fk, fkt = (filter_of(kin_ref, kin_ref.shape[0], flip) for flip in (False, True))
     ez3, ezt = ez3_ref[...], ezt_ref[...]
     eyt = eyt_ref[...]
     halo = max(n_mag, n_kin)
@@ -188,6 +214,7 @@
     plane = G * G
     for x in range(G):
         xs[x * own:(x + 1) * own, :] = psi_ref[:, x * plane:(x + 1) * plane]
+        vrows[x:x + 1, :] = v_ref[:, x * plane:(x + 1) * plane]
 
     def fill(c, value):
         high, low = split(value)
@@ -214,8 +241,8 @@
             ref[at, :] = value
         return finish
 
-    v_first = v_ref[...].astype(BF)
-    v_rest = v_ref[...] - v_first.astype(F32)
+    v_first = vrows[...].astype(BF)
+    v_rest = vrows[...] - v_first.astype(F32)
     v_second = v_rest.astype(BF)
     v_third = (v_rest - v_second.astype(F32)).astype(BF)
     v_stack = jnp.concatenate([v_first, v_second, v_third], axis=0)
@@ -253,18 +280,18 @@
             at = until
 
     h_start()
-    own_h = pltpu.make_async_copy(hbuf.at[me], hc.at[me], lsem.at[1])
+    own_h = pltpu.make_async_copy(hbuf.at[member], hc.at[member], lsem.at[1])
     own_h.start()
 
     own_psi.wait()
     p_arrive()
     for t in range(n):
-        hm[t * own:(t + 1) * own, :] = pc[t]
-    pm_h[...], pm_l[...] = split(hm[...])
+        pf[t * own:(t + 1) * own, :] = pc[t]
+    pm_h[...], pm_l[...] = split(pf[...])
 
     own_h.wait()
     h_arrive()
-    for t in range(n):
+    for t in range(n_half):
         hm[t * own:(t + 1) * own, :] = hc[t]
     h_high, h_low = split(hm[...])
     nt = (((1,), (1,)), ((), ()))
@@ -272,27 +299,27 @@
     def mul_t(left, right):
         return lax.dot_general(left, right, nt, preferred_element_type=F32)
     part = (mul_t(h_high, pm_h[...]) + mul_t(h_high, pm_l[...]) + mul_t(h_low, pm_h[...])) * (1.0 / NC)
-    for t in range(n):
+    for t in range(n_half):
         mp[t] = part[t * own:(t + 1) * own, :]
 
     r_start()
-    own_m = pltpu.make_async_copy(mp.at[me], red.at[me], lsem.at[2])
+    own_m = pltpu.make_async_copy(mp.at[member], red.at[member], lsem.at[2])
     own_m.start()
     own_m.wait()
     r_arrive()
     mrow[...] = jnp.sum(red[...], axis=0)
     b_start()
-    own_r = pltpu.make_async_copy(mrow, mall.at[me], lsem.at[3])
+    own_r = pltpu.make_async_copy(mrow, mall.at[member], lsem.at[3])
     own_r.start()
     own_r.wait()
     b_arrive()
-    margin_t = jnp.concatenate([mall[t] for t in range(n)], axis=0)
+    margin_t = jnp.concatenate([mall[t] for t in range(n_half)], axis=0)
     m_high, m_low = split(margin_t)
     hm[...] = hm[...] - (mul(m_high, pm_h[...]) + mul(m_high, pm_l[...]) + mul(m_low, pm_h[...]))
-    for t in range(n):
+    for t in range(n_half):
         gbuf[t] = hm[t * own:(t + 1) * own, :]
     g_start()
-    own_g = pltpu.make_async_copy(gbuf.at[me], col_slice(out_ref, me), lsem.at[4])
+    own_g = pltpu.make_async_copy(gbuf.at[member], col_slice(out_ref, member), lsem.at[4])
     own_g.start()
     own_g.wait()
     p_sent()
@@ -303,13 +330,11 @@
     g_sent()
 
 
-def shards(n, n_pan, orbitals, potential, magic_taps, kinetic_taps):
+def shards(n_orb, n_pan, orbitals, potential, magic_taps, kinetic_taps):
     own, width = orbitals.shape
-    cols = width // n
+    n, n_half = n_orb * n_pan, n_orb * (n_pan // 2)
+    cols = width // n_half
     rows, total = G * own, n * own
-    magic_matrix = filter_matrix(magic_taps, G)
-    kinetic_matrix = filter_matrix(kinetic_taps, G)
-    mats = jnp.stack([magic_matrix, magic_matrix.T, kinetic_matrix, kinetic_matrix.T])
     n_mag, n_kin = block_range(magic_taps.shape[0]), block_range(kinetic_taps.shape[0])
     halo = max(n_mag, n_kin)
     lane = np.arange(CHUNK)
@@ -323,12 +348,13 @@
     span_m, span_k = (2 * n_mag + 1) * CHUNK, (2 * n_kin + 1) * CHUNK
     chunked = pltpu.VMEM((PARTS * rows, CHUNK), F32)
     halved = pltpu.VMEM(((PARTS + 2 * halo) * rows, CHUNK), BF)
-    blocks = pltpu.VMEM((n, own, cols), F32)
+    smem = pl.BlockSpec(memory_space=pltpu.SMEM)
+    blocks = pltpu.VMEM((n_half, own, cols), F32)
     dma = pltpu.SemaphoreType.DMA
     return pl.pallas_call(
-        functools.partial(kernel, n, n_pan, own, cols, n_mag, n_kin),
+        functools.partial(kernel, n_orb, n_pan, own, cols, n_mag, n_kin),
         out_shape=jax.ShapeDtypeStruct((own, width), F32),
-        in_specs=[vmem] * 10,
+        in_specs=[vmem] * 2 + [smem] * 2 + [vmem] * 7,
         out_specs=pl.BlockSpec(memory_space=OUT_SPACE),
         scratch_shapes=[
             pltpu.VMEM((span_m, CHUNK), BF), pltpu.VMEM((span_m, CHUNK), BF),
@@ -337,17 +363,19 @@
             pltpu.VMEM((4 * rows, rows), BF), pltpu.VMEM((2 * rows, rows), BF), pltpu.VMEM((2 * rows, rows), BF),
             halved, halved,
             pltpu.VMEM((rows, G * G), F32), chunked, chunked, chunked, chunked,
-            blocks, blocks, blocks,
+            pltpu.VMEM((G, G * G), F32),
+            blocks, pltpu.VMEM((n, own, cols), F32), blocks,
             pltpu.VMEM((total, cols), BF), pltpu.VMEM((total, cols), BF), pltpu.VMEM((total, cols), F32),
+            pltpu.VMEM((n_half * own, cols), F32),
             blocks,
-            pltpu.VMEM((n, own, total), F32), pltpu.VMEM((n, own, total), F32),
-            pltpu.VMEM((own, total), F32), pltpu.VMEM((n, own, total), F32),
-            dma((n,)), dma((n,)), dma((n,)), dma((n,)), dma((n,)), dma((n,)), dma((n,)), dma((n,)),
-            dma((n,)), dma((n,)), dma((5,)),
+            pltpu.VMEM((n_half, own, total), F32), pltpu.VMEM((n_half, own, total), F32),
+            pltpu.VMEM((own, total), F32), pltpu.VMEM((n_half, own, total), F32),
+            dma((n,)), dma((n,)), dma((n_half,)), dma((n_half,)), dma((n_half,)), dma((n_half,)), dma((n_half,)),
+            dma((n_half,)), dma((n_half,)), dma((n_half,)), dma((5,)),
         ],
         compiler_params=pltpu.CompilerParams(
             collective_id=0, has_side_effects=True, vmem_limit_bytes=60 * 1024 * 1024),
-    )(orbitals, potential.reshape(G, G * G), mats, ez3, ezt, ey3, eyt, ex3, ext, same)
+    )(orbitals, potential.reshape(1, width), magic_taps, kinetic_taps, ez3, ezt, ey3, eyt, ex3, ext, same)
 
 
 OUT_SPACE = pl.ANY
@@ -356,9 +384,9 @@
 def solution(mesh):
     placed = (P(("orb", "pan"), None), P(), P(), P())
     n_pan = mesh.shape["pan"]
-    n = mesh.shape["orb"] * n_pan
-    aligned = NC % (n * 128) == 0
-    body = functools.partial(shards, n, n_pan) if aligned else plain_shards
+    n_orb = mesh.shape["orb"]
+    aligned = n_pan % 2 == 0 and NC % (n_orb * (n_pan // 2) * 128) == 0
+    body = functools.partial(shards, n_orb, n_pan) if aligned else plain_shards
     return jax.shard_map(
         body, mesh=mesh, in_specs=placed, out_specs=P(("orb", "pan"), None), check_vma=False
     )

time: 150 us -> 129 us (0.86)
  Pallas kernels: 142 us -> 126 us
  other arithmetic: 2.83 us -> 0 us
  local copies, waits for them, and re-layouts: 4.79 us -> 2.8 us
    pallas_call x1, Pallas kernels: 142 us -> 126 us  [shards(): pl.pallas_call(functools.partial(kernel, n_orb, n_pan, own, cols, n_mag,...]
    reduce_sum x2 -> x0, other arithmetic: 2.16 us -> none  [filter_matrix(): jnp.sum(jnp.where(offset == 0, tap_values[:, None, None], jnp.float32(0.0...]
    reshape x1 -> x0, local copies, waits for them, and re-layouts: 1.85 us -> none  [shards(): potential.reshape(G, G * G)]
where the time goes in v1:
time: 129 us
  Pallas kernels  126 us (98%)
  local copies, waits for them, and re-layouts  2.8 us (2%)
    pallas_call x1, Pallas kernels, shards(): pl.pallas_call(functools.partial(kernel, n_orb, n_pan, own, cols, n_mag,...  126 us
    unnamed x1, local copies, waits for them, and re-layouts  2.8 us

profile of v1, /device:TPU:0, one launch (start us, length us, event | category | flops | bytes accessed | tf_op | source)
XLA Modules:
  0.0 128.5 jit_solution(8901921722477245855)
XLA Ops:
  0.0 125.7 %shard_map.145 = f32[4,110592]{1,0:T(4,128)} custom-call(f32[4,110592]{1,0:T(4,128)} %psi_ref.1, f32[1,110592]{1,0:T(1,128)} %bitcast.1, f32[16]{0:T(128)} %mag_ref.1, f32[29]{0:T(128)} %kin_ref.1, bf16[384,144]{1,0:T(8,128)(2,1)} %constant.22.clone.ez3_ref, bf16[48,384]{1,0:T(8,128)(2,1)} %constant.34.ezt_ref, bf16[5,384,144]{2,1,0:T(8,128)(2,1)} %constant.40.ey3_ref, ...), custom_call_target="tpu_custom_call" | custom-call | tf_op jit(solution)/shard_map/pallas_call | solution.py:354
  125.7 2.8 %copy.17 = f32[4,110592]{1,0:T(4,128)} copy(f32[4,110592]{1,0:T(4,128)} %shard_map.145) | data formatting | bytes 3538944

commit v2 on v1

--- a/solution.py
+++ b/solution.py
@@ -1,4 +1,5 @@
 import functools
+import math
 
 import jax
 import jax.numpy as jnp
@@ -117,11 +118,11 @@
     return total
 
 
-def kernel(n_orb, n_pan, own, cols, n_mag, n_kin,
+def kernel(n_orb, n_pan, own, cols, n_mag, n_kin, pieces, per_tile,
            psi_ref, v_ref, mag_ref, kin_ref, ez3_ref, ezt_ref, ey3_ref, eyt_ref, ex3_ref, ext_ref, same_ref,
            out_ref,
            wfh, wfl, wbh, wbl, wkh, wkl, xl1, xl2, xb1, sh, sl, xs, kx, kyz, tt, vs, vrows,
-           hbuf, pc, hc, pm_h, pm_l, pf, hm, gbuf, mp, red, mrow, mall,
+           psi_vm, hbuf, pc, hc, pm_h, pm_l, pf, hm, hs, gbuf, mp, red, mrow, mall,
            psend, precv, hsend, hrecv, rsend, rrecv, bsend, brecv, gsend, grecv, lsem):
     half = n_pan // 2
     n, n_half = n_orb * n_pan, n_orb * half
@@ -142,10 +143,8 @@
         return lax.div(t, n_pan) * half + lax.rem(lax.rem(t, n_pan), half)
 
     def each(action, count=n, first=me):
-        def step(k, carry):
+        for k in range(1, count):
             action(lax.rem(first + k, count))
-            return carry
-        lax.fori_loop(1, count, step, 0)
 
     def sender(src, dst, send, recv, count=n_half, mine=member, coords=at_half):
         def copy(t):
@@ -164,20 +163,37 @@
     def col_slice(ref, block):
         return ref.at[:, pl.ds(pl.multiple_of(block * cols, 128), cols)]
 
+    load = pltpu.make_async_copy(psi_ref, psi_vm, lsem.at[0])
+    load.start()
     barrier = pltpu.get_barrier_semaphore()
     each(lambda t: pl.semaphore_signal(barrier, inc=1, device_id=at_all(t), device_id_type=pl.DeviceIdType.MESH))
     pl.semaphore_wait(barrier, n - 1)
 
-    p_start, p_arrive, p_sent = sender(
-        lambda t: col_slice(psi_ref, block_of(t)), lambda t: pc.at[t], psend, precv, n, me, at_all)
+    def psi_copy(k):
+        t = lax.rem(me + k, n)
+        return pltpu.make_async_remote_copy(
+            src_ref=col_slice(psi_ref, block_of(t)), dst_ref=pc.at[n - k], send_sem=psend.at[k],
+            recv_sem=precv.at[n - k], device_id=at_all(t), device_id_type=pl.DeviceIdType.MESH)
+
+    def p_start():
+        for k in range(1, n):
+            psi_copy(k).start()
+
+    def p_sent():
+        for k in range(1, n):
+            psi_copy(k).wait_send()
     h_start, h_arrive, h_sent = sender(lambda t: hbuf.at[t], lambda t: hc.at[t], hsend, hrecv)
     r_start, r_arrive, r_sent = sender(lambda t: mp.at[t], lambda t: red.at[t], rsend, rrecv)
     b_start, b_arrive, b_sent = sender(lambda t: mrow, lambda t: mall.at[t], bsend, brecv)
-    g_start, g_arrive, g_sent = sender(lambda t: gbuf.at[t], lambda t: col_slice(out_ref, t), gsend, grecv)
+    wide = cols // pieces
+    g_pieces = [
+        sender(lambda t, c=c: gbuf.at[c, t],
+               lambda t, c=c: out_ref.at[:, pl.ds(pl.multiple_of(t * cols + c * wide, 128), wide)],
+               gsend.at[c], grecv.at[c]) for c in range(pieces)]
 
     p_start()
-    own_psi = pltpu.make_async_copy(col_slice(psi_ref, member), pc.at[me], lsem.at[0])
-    own_psi.start()
+    load.wait()
+    pc[0] = psi_vm[:, pl.ds(pl.multiple_of(member * cols, 128), cols)]
 
     fm, fmt = (filter_of(mag_ref, mag_ref.shape[0], flip) for flip in (False, True))
     fk, fkt = (filter_of(kin_ref, kin_ref.shape[0], flip) for flip in (False, True))
@@ -213,7 +229,7 @@
 
     plane = G * G
     for x in range(G):
-        xs[x * own:(x + 1) * own, :] = psi_ref[:, x * plane:(x + 1) * plane]
+        xs[x * own:(x + 1) * own, :] = psi_vm[:, x * plane:(x + 1) * plane]
         vrows[x:x + 1, :] = v_ref[:, x * plane:(x + 1) * plane]
 
     def fill(c, value):
@@ -283,51 +299,67 @@
     own_h = pltpu.make_async_copy(hbuf.at[member], hc.at[member], lsem.at[1])
     own_h.start()
 
-    own_psi.wait()
-    p_arrive()
-    for t in range(n):
-        pf[t * own:(t + 1) * own, :] = pc[t]
-    pm_h[...], pm_l[...] = split(pf[...])
-
+    def take(group):
+        for r in range(group * per_tile, (group + 1) * per_tile):
+            if r > 0:
+                psi_copy(n - r).wait_recv()
+        for r in range(group * per_tile, (group + 1) * per_tile):
+            pf[(r % per_tile) * own:(r % per_tile + 1) * own, :] = pc[r]
+        at = slice(group * per_tile * own, (group + 1) * per_tile * own)
+        pm_h[at, :], pm_l[at, :] = split(pf[...])
+
+    groups = n // per_tile
+    for group in range(groups - 1, 0, -1):
+        take(group)
     own_h.wait()
     h_arrive()
     for t in range(n_half):
         hm[t * own:(t + 1) * own, :] = hc[t]
-    h_high, h_low = split(hm[...])
+    half_rows = n_half * own
+    hs[:half_rows, :], hs[half_rows:, :] = split(hm[...])
+    take(0)
     nt = (((1,), (1,)), ((), ()))
 
     def mul_t(left, right):
         return lax.dot_general(left, right, nt, preferred_element_type=F32)
-    part = (mul_t(h_high, pm_h[...]) + mul_t(h_high, pm_l[...]) + mul_t(h_low, pm_h[...])) * (1.0 / NC)
+    both = mul_t(hs[...], pm_h[...])
+    part = (both[:half_rows] + both[half_rows:] + mul_t(hs[:half_rows, :], pm_l[...])) * (1.0 / NC)
+    part = pltpu.roll(part, me * own, 1)
     for t in range(n_half):
         mp[t] = part[t * own:(t + 1) * own, :]
 
     r_start()
-    own_m = pltpu.make_async_copy(mp.at[member], red.at[member], lsem.at[2])
-    own_m.start()
-    own_m.wait()
+    red[member] = mp[member]
     r_arrive()
     mrow[...] = jnp.sum(red[...], axis=0)
     b_start()
-    own_r = pltpu.make_async_copy(mrow, mall.at[member], lsem.at[3])
-    own_r.start()
-    own_r.wait()
+    mall[member] = mrow[...]
     b_arrive()
     margin_t = jnp.concatenate([mall[t] for t in range(n_half)], axis=0)
-    m_high, m_low = split(margin_t)
-    hm[...] = hm[...] - (mul(m_high, pm_h[...]) + mul(m_high, pm_l[...]) + mul(m_low, pm_h[...]))
-    for t in range(n_half):
-        gbuf[t] = hm[t * own:(t + 1) * own, :]
-    g_start()
-    own_g = pltpu.make_async_copy(gbuf.at[member], col_slice(out_ref, member), lsem.at[4])
-    own_g.start()
-    own_g.wait()
+    margin_t = pltpu.roll(margin_t, lax.rem(total - me * own, total), 1)
+    m_both = jnp.concatenate(split(margin_t), axis=0)
+    own_g = []
+    for c in range(pieces):
+        lanes = slice(c * wide, (c + 1) * wide)
+        turned = mul(m_both, pm_h[:, lanes])
+        value = hm[:, lanes] - (
+            turned[:half_rows] + turned[half_rows:] + mul(m_both[:half_rows], pm_l[:, lanes]))
+        for t in range(n_half):
+            gbuf[c, t] = value[t * own:(t + 1) * own, :]
+        g_pieces[c][0]()
+        copy = pltpu.make_async_copy(
+            gbuf.at[c, member], out_ref.at[:, pl.ds(pl.multiple_of(member * cols + c * wide, 128), wide)],
+            lsem.at[2 + c])
+        copy.start()
+        own_g.append(copy)
     p_sent()
     h_sent()
     r_sent()
     b_sent()
-    g_arrive()
-    g_sent()
+    for c in range(pieces):
+        own_g[c].wait()
+        g_pieces[c][1]()
+        g_pieces[c][2]()
 
 
 def shards(n_orb, n_pan, orbitals, potential, magic_taps, kinetic_taps):
@@ -335,6 +367,8 @@
     n, n_half = n_orb * n_pan, n_orb * (n_pan // 2)
     cols = width // n_half
     rows, total = G * own, n * own
+    pieces = 3 if cols % (3 * 128) == 0 else 1
+    per_tile = math.gcd(n, -(-16 // own))
     n_mag, n_kin = block_range(magic_taps.shape[0]), block_range(kinetic_taps.shape[0])
     halo = max(n_mag, n_kin)
     lane = np.arange(CHUNK)
@@ -352,9 +386,9 @@
     blocks = pltpu.VMEM((n_half, own, cols), F32)
     dma = pltpu.SemaphoreType.DMA
     return pl.pallas_call(
-        functools.partial(kernel, n_orb, n_pan, own, cols, n_mag, n_kin),
+        functools.partial(kernel, n_orb, n_pan, own, cols, n_mag, n_kin, pieces, per_tile),
         out_shape=jax.ShapeDtypeStruct((own, width), F32),
-        in_specs=[vmem] * 2 + [smem] * 2 + [vmem] * 7,
+        in_specs=[pl.BlockSpec(memory_space=pl.ANY), vmem] + [smem] * 2 + [vmem] * 7,
         out_specs=pl.BlockSpec(memory_space=OUT_SPACE),
         scratch_shapes=[
             pltpu.VMEM((span_m, CHUNK), BF), pltpu.VMEM((span_m, CHUNK), BF),
@@ -364,14 +398,14 @@
             halved, halved,
             pltpu.VMEM((rows, G * G), F32), chunked, chunked, chunked, chunked,
             pltpu.VMEM((G, G * G), F32),
-            blocks, pltpu.VMEM((n, own, cols), F32), blocks,
-            pltpu.VMEM((total, cols), BF), pltpu.VMEM((total, cols), BF), pltpu.VMEM((total, cols), F32),
-            pltpu.VMEM((n_half * own, cols), F32),
-            blocks,
+            pltpu.VMEM((own, width), F32), blocks, pltpu.VMEM((n, own, cols), F32), blocks,
+            pltpu.VMEM((total, cols), BF), pltpu.VMEM((total, cols), BF), pltpu.VMEM((per_tile * own, cols), F32),
+            pltpu.VMEM((n_half * own, cols), F32), pltpu.VMEM((2 * n_half * own, cols), BF),
+            pltpu.VMEM((pieces, n_half, own, cols // pieces), F32),
             pltpu.VMEM((n_half, own, total), F32), pltpu.VMEM((n_half, own, total), F32),
             pltpu.VMEM((own, total), F32), pltpu.VMEM((n_half, own, total), F32),
             dma((n,)), dma((n,)), dma((n_half,)), dma((n_half,)), dma((n_half,)), dma((n_half,)), dma((n_half,)),
-            dma((n_half,)), dma((n_half,)), dma((n_half,)), dma((5,)),
+            dma((n_half,)), dma((pieces, n_half)), dma((pieces, n_half)), dma((2 + pieces,)),
         ],
         compiler_params=pltpu.CompilerParams(
             collective_id=0, has_side_effects=True, vmem_limit_bytes=60 * 1024 * 1024),

time: 129 us -> 125 us (0.969)
  Pallas kernels: 126 us -> 122 us
    pallas_call x1, Pallas kernels: 126 us -> 122 us  [shards(): pl.pallas_call(functools.partial(kernel, n_orb, n_pan, own, cols, n_mag,...]
where the time goes in v2:
time: 125 us
  Pallas kernels  122 us (98%)
  local copies, waits for them, and re-layouts  2.8 us (2%)
    pallas_call x1, Pallas kernels, shards(): pl.pallas_call(functools.partial(kernel, n_orb, n_pan, own, cols, n_mag,...  122 us
    unnamed x1, local copies, waits for them, and re-layouts  2.8 us

profile of v2, /device:TPU:0, one launch (start us, length us, event | category | flops | bytes accessed | tf_op | source)
XLA Modules:
  0.0 124.9 jit_solution(17929289223740459428)
XLA Ops:
  0.0 122.1 %shard_map.145 = f32[4,110592]{1,0:T(4,128)} custom-call(f32[4,110592]{1,0:T(4,128)} %psi_ref.1, f32[1,110592]{1,0:T(1,128)} %bitcast.1, f32[16]{0:T(128)} %mag_ref.1, f32[29]{0:T(128)} %kin_ref.1, bf16[384,144]{1,0:T(8,128)(2,1)} %constant.22.clone.ez3_ref, bf16[48,384]{1,0:T(8,128)(2,1)} %constant.34.ezt_ref, bf16[5,384,144]{2,1,0:T(8,128)(2,1)} %constant.40.ey3_ref, ...), custom_call_target="tpu_custom_call" | custom-call | tf_op jit(solution)/shard_map/pallas_call | solution.py:388
  122.1 2.8 %copy.17 = f32[4,110592]{1,0:T(4,128)} copy(f32[4,110592]{1,0:T(4,128)} %shard_map.145) | data formatting | bytes 3538944
